TPU v7x, 1024 devices: a whole 8x8x8 slice. The times are simulated.
1024 devices in a mesh: stn: 256 (over y_lo, z, x, core), elem: 4 (over y_hi).
Axes of the slice: x: 8, y: 8 (y_hi: 4, y_lo: 2; y = y_hi * 2 + y_lo), z: 8, core: 2. Of those that a mesh axis runs over, the one named last changes fastest.
Arguments:
- voltages: bfloat16 [2, 256, 64, 16, 128], P(None, 'stn', 'elem'), may hold values from -6 to 6
- weights: bfloat16 [2, 8, 64, 16], P(None, None, 'elem'), may hold values from -0.5 to 0.5
Outputs:
- spectra: float32 [2, 16, 2048, 2048], P(None, 'elem', 'stn')
All inputs are finite; a program needn't handle non-finite values.
Results may differ from a plain program's by a relative error of at most 0.0075.
Values may be sent and summed in bfloat16 or wider, within the bound.
A program may use at most 32 MiB of HBM per device.

v0:
```python
import jax
import jax.numpy as jnp
from jax import lax
from jax.sharding import PartitionSpec as P


def form_beams(voltages, weights):
    real_part = jnp.einsum(
        "kec,sect->sckt", weights[0], voltages[0], preferred_element_type=jnp.float32
    ) + jnp.einsum("kec,sect->sckt", weights[1], voltages[1], preferred_element_type=jnp.float32)
    imag_part = jnp.einsum(
        "kec,sect->sckt", weights[0], voltages[1], preferred_element_type=jnp.float32
    ) - jnp.einsum("kec,sect->sckt", weights[1], voltages[0], preferred_element_type=jnp.float32)
    return jnp.stack([real_part, imag_part])


def row_folder(mine, piece):
    spec_real = jnp.einsum(
        "cit,cjt->cij", mine[0], piece[0], preferred_element_type=jnp.float32
    ) + jnp.einsum("cit,cjt->cij", mine[1], piece[1], preferred_element_type=jnp.float32)
    spec_imag = jnp.einsum(
        "cit,cjt->cij", mine[1], piece[0], preferred_element_type=jnp.float32
    ) - jnp.einsum("cit,cjt->cij", mine[0], piece[1], preferred_element_type=jnp.float32)
    return jnp.stack([spec_real, spec_imag])


def body(voltages, weights):
    partial_beams = form_beams(voltages, weights)
    samples = voltages.shape[4]
    summed = lax.psum_scatter(partial_beams, "elem", scatter_dimension=2, tiled=True)
    mine = summed.astype(jnp.bfloat16)[:, 0]
    spectra = row_folder(mine, lax.all_gather(mine, "stn", axis=2, tiled=True))
    return spectra / jnp.float32(samples)


def solution(mesh):
    placed = (P(None, "stn", "elem", None, None), P(None, None, "elem", None))
    return jax.shard_map(
        body, mesh=mesh, in_specs=placed, out_specs=P(None, "elem", "stn", None), check_vma=False
    )
```

profile of v0, /device:TPU:1, one launch (start us, length us, event | category | flops | bytes accessed | tf_op | source)
XLA Modules:
  0.0 466.6 jit_solution(8107558861760587658)
XLA Ops:
  6.5 0.0 all-gather.3.cloned.1.call-start
  6.5 0.8 fusion.13
  7.3 0.1 copy.16
  7.4 0.1 copy.14
  7.5 0.9 fusion.12
  8.4 0.1 fusion.6
  8.5 0.1 fusion.7
  8.7 0.2 fusion.5
  8.8 0.1 fusion.4
  9.0 20.1 %all-reduce.2 = bf16[2,1,16,8,128]{4,3,2,1,0:T(8,128)(2,1)S(1)} all-reduce(f32[2,1,16,8,128]{4,3,2,1,0:T(8,128)S(1)} %pad_maximum_fusion), channel_id=3, replica_groups=mesh['stn'=256,'elem'=4] {'elem'}, use_global_device_ids=true, to_apply=%region_0.0.clone | all-reduce | flops 32768 | bytes 196608
  29.1 1.3 dynamic-slice
  31.1 0.6 dynamic-slice_convert_fusion
  31.7 0.0 copy-start.1
  31.7 0.0 all-gather.3.cloned.1.call-update
  31.7 421.2 %all-gather.3.cloned.1.call-done = bf16[2,1,4,2048,128]{4,3,2,1,0:T(8,128)(2,1)} async-done(((bf16[2,1,4,8,128]{4,3,2,1,0:T(8,128)(2,1)}), bf16[2,1,4,2048,128]{4,3,2,1,0:T(8,128)(2,1)}) %all-gather.3.cloned.1.call-update) | async-done | bytes 4194320 | tf_op jit(solution)/shard_map/all_gather | solution.py:32
  452.9 0.0 copy-start
  452.9 2.4 fusion.2
  455.3 2.3 fusion.3
  457.6 0.0 copy-done.1
  457.6 0.0 copy-done
  457.6 0.7 fusion
  458.2 0.7 fusion.1
  458.9 0.9 maximum_multiply_fusion
  (1 shorter events, 0.0 us)
Async XLA Ops:
  6.5 446.4 %all-gather.3.cloned.1.call-start = ((), (), s32[]{:S(2)}) async-start(), calls=%async_computation | async-start | bytes 4210688 | tf_op jit(solution)/shard_map/all_gather | solution.py:32
  31.7 425.9 %copy-start.1 = (bf16[2,1,4,8,128]{4,3,2,1,0:T(8,128)(2,1)S(1)}, bf16[2,1,4,8,128]{4,3,2,1,0:T(8,128)(2,1)}, u32[]{:S(2)}) copy-start(bf16[2,1,4,8,128]{4,3,2,1,0:T(8,128)(2,1)} %dynamic-slice_convert_fusion) | copy-start | bytes 49156
  452.9 4.7 copy-start
Sparse Core Ops, SparseCore 0:
  31.8 421.0 all-gather.2
where the time goes:
time: 467 us
  waiting for transfers between devices  421 us (90%)
  blocking collectives  20.1 us (4%)
  between operations  14.1 us (3%)
  matrix products  6.55 us (1%)
    all_gather x1, waiting for transfers between devices, body(): spectra = row_folder(mine, lax.all_gather(mine, 'stn', axis=2, tiled=True))  421 us
    unnamed x1, blocking collectives  20.1 us
  transfers between devices with their start and end apart: 1, of which 1 were waited for; matrix products, arithmetic and copies ran while one was open for 0% of the time, Pallas kernels for 0%

commit v1 on v0

v1 whole, which is shorter than its diff:
```python
import functools

import jax
import jax.numpy as jnp
from jax import lax
from jax.experimental import pallas as pl
from jax.experimental.pallas import tpu as pltpu
from jax.sharding import PartitionSpec as P

MESH = pl.DeviceIdType.MESH
F32, BF16 = jnp.float32, jnp.bfloat16
RING, YS, CORES, PARTS = 8, 2, 2, 4
NB, CH, HALF = 8, 16, 2
PLANE = YS * RING
FAR = (4, 3, 5, 2, 6, 1, 7)


def iota(shape, dim):
    return lax.broadcasted_iota(jnp.int32, shape, dim)


def beam_matrix(w_ref):
    elems = w_ref.shape[1] // NB
    spread = (iota((CH, elems * CH), 1) % CH == iota((CH, elems * CH), 0)).astype(F32).astype(BF16)
    shape = (NB * elems, elems * CH)
    own = iota(shape, 0) % elems == iota(shape, 1) // CH
    shape = (2 * NB, NB * elems)
    pick = (iota(shape, 0) % NB == iota(shape, 1) // elems).astype(F32).astype(BF16)
    flat = []
    for part in range(2):
        wide = jnp.dot(w_ref[part], spread, preferred_element_type=F32)
        wide = jnp.where(own, wide, 0.0).astype(BF16)
        flat.append(jnp.dot(pick, wide, preferred_element_type=F32))
    top = iota(flat[0].shape, 0) < NB
    left = jnp.where(top, flat[0], -flat[1])
    right = jnp.where(top, flat[1], flat[0])
    both = jnp.concatenate([left, right], axis=1)
    lane = iota(both.shape, 1) % CH
    return jnp.concatenate(
        [jnp.where(lane == c, both, 0.0).astype(BF16) for c in range(CH)], axis=0
    )


def kernel(scale, volt_hbm, w_hbm, out_ref, volt, w, part32, part16, got, mine, cols, rows, res, ret,
           in_sem, es_sem, er_sem, gs_sem, cr_sem, rr_sem, ts_sem, tr_sem):
    s, e = lax.axis_index("stn"), lax.axis_index("elem")
    k, x = lax.rem(s, 2), lax.rem(s // 2, RING)
    z, y = lax.rem(s // (2 * RING), RING), s // (2 * RING * RING)

    def at(yy, zz, xx, kk):
        return {"stn": ((yy * RING + zz) * RING + xx) * 2 + kk, "elem": e}

    def on_ring(h, d, kk):
        return at(y, z, lax.rem(x + d, RING), kk) if h == 0 else at(y, lax.rem(z + d, RING), x, kk)

    def on_plane(h, dy, d, kk):
        yy = lax.rem(y + dy, YS)
        if h == 0:
            return at(yy, lax.rem(z + d, RING), x, kk)
        return at(yy, z, lax.rem(x + d, RING), kk)

    r_own, w_own = x + k * (z - x), z + k * (x - z)

    def my_plane(dy, d, kk):
        yy = lax.rem(y + dy, YS)
        ww = lax.rem(w_own + d, RING)
        return at(yy, ww + k * (z - ww), x + k * (ww - x), kk)

    def my_ring(d, kk):
        rr = lax.rem(r_own + d, RING)
        return at(y, z + k * (rr - z), rr + k * (x - rr), kk)

    partner = at(y, z, x, 1 - k)
    plane_steps = [(dy, d) for dy in (1, 0) for d in FAR + (0,) if (dy, d) != (0, 0)]

    barrier = pltpu.get_barrier_semaphore()
    peers = 0

    def greet(device):
        nonlocal peers
        pl.semaphore_signal(barrier, inc=1, device_id=device, device_id_type=MESH)
        peers += 1

    for d in range(1, PARTS):
        greet({"stn": s, "elem": lax.rem(e + d, PARTS)})
    greet(partner)
    for dy, d in plane_steps:
        greet(my_plane(dy, d, k))
        greet(my_plane(dy, d, 1 - k))
    for dy, d in plane_steps:
        yy = lax.rem(y + dy, YS)
        rr = lax.rem(r_own + d, RING)
        greet(at(yy, z + k * (rr - z), rr + k * (x - rr), 1 - k))
    for d in FAR:
        greet(my_ring(d, k))

    load_v = pltpu.make_async_copy(volt_hbm, volt, in_sem.at[0])
    load_w = pltpu.make_async_copy(w_hbm, w, in_sem.at[1])
    load_w.start()
    load_v.start()
    load_w.wait()
    matrix = beam_matrix(w)
    load_v.wait()
    partial = jnp.dot(matrix, volt[...], preferred_element_type=F32)
    part32[...] = partial
    part16[...] = partial.astype(part16.dtype)
    pl.semaphore_wait(barrier, peers)

    quarter = part32.shape[0] // PARTS
    sends = []
    for d in (2, 1, 3):
        q = lax.rem(e + d, PARTS)
        copy = pltpu.make_async_remote_copy(
            src_ref=part16.at[pl.ds(pl.multiple_of(q * quarter, quarter), quarter)],
            dst_ref=got.at[d - 1],
            send_sem=es_sem.at[d - 1],
            recv_sem=er_sem.at[d - 1],
            device_id={"stn": s, "elem": q},
            device_id_type=MESH,
        )
        copy.start()
        sends.append(copy)
    total = part32[pl.ds(pl.multiple_of(e * quarter, quarter), quarter)]
    for copy, d in zip(sends, (2, 1, 3)):
        copy.wait_recv()
    for d in (1, 2, 3):
        total = total + got[d - 1].astype(F32)
    beams = total.astype(BF16).reshape(mine.shape)
    mine[...] = beams

    count = 0

    def send(src, dst, sem, device):
        nonlocal count
        copy = pltpu.make_async_remote_copy(
            src_ref=src, dst_ref=dst, send_sem=gs_sem.at[count], recv_sem=sem,
            device_id=device, device_id_type=MESH,
        )
        copy.start()
        sends.append(copy)
        count += 1

    coord = ((x, z), (z, x))
    for d in FAR:
        for h in range(2):
            slot = coord[h][0] * 2 + k
            send(mine.at[h], cols.at[slot], cr_sem.at[slot], on_ring(h, d, h))
    for dy, d in plane_steps:
        for h in range(2):
            slot = (y * RING + coord[h][1]) * 2 + k
            send(mine.at[h], rows.at[slot], rr_sem.at[slot], on_plane(h, dy, d, h))
    slot = w_own * 2 + k
    send(mine.at[1 - k], cols.at[slot], cr_sem.at[slot], partner)
    slot = (y * RING + r_own) * 2 + k
    send(mine.at[1 - k], rows.at[slot], rr_sem.at[slot], partner)
    own = mine[k]
    own_col, own_row = r_own * 2, (y * RING + w_own) * 2
    cols[own_col + k] = own
    rows[own_row + k] = own

    def landed(dst, sem):
        pltpu.make_async_remote_copy(
            src_ref=dst, dst_ref=dst, send_sem=gs_sem.at[0], recv_sem=sem,
            device_id=partner, device_id_type=MESH,
        ).wait_recv()

    landed(cols.at[own_col + 1 - k], cr_sem.at[own_col + 1 - k])
    for d in range(1, RING):
        for kk in range(2):
            slot = lax.rem(r_own + d, RING) * 2 + kk
            landed(cols.at[slot], cr_sem.at[slot])
    col_parts = []
    for c in range(HALF):
        wide = cols[:, c].astype(F32).reshape(RING * CORES, 2, NB, -1)
        col_parts.append(tuple(
            wide[:, part].reshape(RING * CORES * NB, -1).astype(BF16) for part in range(2)
        ))

    back = 0
    for dy in range(YS):
        yy = lax.rem(y + dy, YS)
        base = yy * RING * CORES
        for d in range(RING):
            slot = base + lax.rem(w_own + d, RING) * 2
            if (dy, d) == (0, 0):
                landed(rows.at[slot + 1 - k], rr_sem.at[slot + 1 - k])
            else:
                for kk in range(2):
                    landed(rows.at[slot + kk], rr_sem.at[slot + kk])
        block = pl.ds(base, RING * CORES)
        for c in range(HALF):
            tile = rows[block, c]
            n, _, samples = tile.shape
            wide = tile.astype(F32).reshape(n, 2, NB, samples)
            turned = jnp.concatenate([wide[:, 1:], -wide[:, :1]], axis=1)
            turned = turned.reshape(n * 2 * NB, samples).astype(BF16)
            tile = tile.reshape(n * 2 * NB, samples)
            cross = (((1,), (1,)), ((), ()))
            prod = lax.dot_general(tile, col_parts[c][0], cross, preferred_element_type=F32)
            prod += lax.dot_general(turned, col_parts[c][1], cross, preferred_element_type=F32)
            res[block, c] = (prod * scale).astype(BF16).reshape(n, 2 * NB, -1)
        here = y * RING + w_own
        for d in FAR + (0,):
            slot = base + lax.rem(w_own + d, RING) * 2
            if (dy, d) == (0, 0):
                kinds = (1 - k,)
            else:
                kinds = (0, 1)
            for kk in kinds:
                copy = pltpu.make_async_remote_copy(
                    src_ref=res.at[slot + kk], dst_ref=ret.at[k, here], send_sem=ts_sem.at[back],
                    recv_sem=tr_sem.at[k, here], device_id=my_plane(dy, d, kk), device_id_type=MESH,
                )
                copy.start()
                sends.append(copy)
                back += 1
        if dy == 0:
            ret[k, here] = res[base + w_own * 2 + k]

    for dy, d in [(0, 0)] + plane_steps[::-1]:
        pos = lax.rem(y + dy, YS) * RING
        mine_at, other_at = pos + lax.rem(w_own + d, RING), pos + lax.rem(r_own + d, RING)
        if (dy, d) != (0, 0):
            landed(ret.at[k, mine_at], tr_sem.at[k, mine_at])
        landed(ret.at[1 - k, other_at], tr_sem.at[1 - k, other_at])

    lanes = out_ref.shape[3] // PLANE
    for pos in range(PLANE):
        for c in range(HALF):
            tile = ret[0, pos, c].astype(F32)
            for part in range(2):
                out_ref[part, c, :, pl.ds(pos * lanes, lanes)] = tile[part * NB:(part + 1) * NB]
    group = iota((2 * NB, lanes), 1) // (CORES * NB)
    for yy in range(YS):
        for c in range(HALF):
            tiles = [ret[1, yy * RING + i, c].astype(F32) for i in range(RING)]
            for bit in (1, 2, 4):
                high = (group // bit) % 2 == 1
                swapped = list(tiles)
                for i in range(RING):
                    if i & bit:
                        continue
                    a, b = tiles[i], tiles[i | bit]
                    shift = bit * CORES * NB
                    swapped[i] = jnp.where(high, pltpu.roll(b, shift, 1), a)
                    swapped[i | bit] = jnp.where(high, b, pltpu.roll(a, lanes - shift, 1))
                tiles = swapped
            for i in range(RING):
                for part in range(2):
                    out_ref[part, HALF + c, :, pl.ds((yy * RING + i) * lanes, lanes)] = (
                        tiles[i][part * NB:(part + 1) * NB]
                    )
    for copy in sends:
        copy.wait_send()


def body(voltages, weights):
    samples = voltages.shape[4]
    elems = voltages.shape[2]
    mine_ch = CH // PARTS
    devices = PLANE * RING * CORES
    volt = voltages.reshape(2 * elems * CH, samples)
    w = weights.reshape(2, NB * elems, CH)
    lanes = RING * CORES * NB
    gathers = 2 * (RING - 1) + 2 * (PLANE - 1) + 2
    return pl.pallas_call(
        functools.partial(kernel, 1.0 / samples),
        out_shape=jax.ShapeDtypeStruct((2, mine_ch, NB, devices * NB), F32),
        in_specs=[pl.BlockSpec(memory_space=pl.ANY)] * 2,
        out_specs=pl.BlockSpec(memory_space=pltpu.VMEM),
        scratch_shapes=[
            pltpu.VMEM(volt.shape, BF16),
            pltpu.VMEM(w.shape, BF16),
            pltpu.VMEM((CH * 2 * NB, samples), F32),
            pltpu.VMEM((CH * 2 * NB, samples), BF16),
            pltpu.VMEM((PARTS - 1, mine_ch * 2 * NB, samples), BF16),
            pltpu.VMEM((2, HALF, 2 * NB, samples), BF16),
            pltpu.VMEM((RING * CORES, HALF, 2 * NB, samples), BF16),
            pltpu.VMEM((PLANE * CORES, HALF, 2 * NB, samples), BF16),
            pltpu.VMEM((PLANE * CORES, HALF, 2 * NB, lanes), BF16),
            pltpu.VMEM((2, PLANE, HALF, 2 * NB, lanes), BF16),
            pltpu.SemaphoreType.DMA((2,)),
            pltpu.SemaphoreType.DMA((PARTS - 1,)),
            pltpu.SemaphoreType.DMA((PARTS - 1,)),
            pltpu.SemaphoreType.DMA((gathers,)),
            pltpu.SemaphoreType.DMA((RING * CORES,)),
            pltpu.SemaphoreType.DMA((PLANE * CORES,)),
            pltpu.SemaphoreType.DMA((PLANE * CORES,)),
            pltpu.SemaphoreType.DMA((2, PLANE)),
        ],
        compiler_params=pltpu.CompilerParams(collective_id=0, has_side_effects=True),
    )(volt, w)


def solution(mesh):
    placed = (P(None, "stn", "elem", None, None), P(None, None, "elem", None))
    return jax.shard_map(
        body, mesh=mesh, in_specs=placed, out_specs=P(None, "elem", "stn", None), check_vma=False
    )
```

time: 467 us -> 45.8 us (0.10)
  waiting for transfers between devices: 421 us -> 0 us
  Pallas kernels: 0 us -> 43.8 us
  blocking collectives: 20.1 us -> 0 us
  between operations: 14.1 us -> 0.01 us
  matrix products: 6.55 us -> 0 us
    all_gather x1 -> x0, waiting for transfers between devices: 421 us -> none  [body(): spectra = row_folder(mine, lax.all_gather(mine, 'stn', axis=2, tiled=True))]
    pallas_call x0 -> x1, Pallas kernels: none -> 43.8 us  [body(): pl.pallas_call(functools.partial(kernel, 1.0 / samples), out_shape=jax.Sh...]
    unnamed x1 -> x0, blocking collectives: 20.1 us -> none
    dot_general x8 -> x0, matrix products: 6.55 us -> none  [the longest x1 2.39 us: row_folder(): jnp.einsum('cit,cjt->cij', mine[1], piece[0], preferred_element_type=jnp....]
  transfers between devices with their start and end apart: 1 -> 0, of which waited for: 1 -> 0; matrix products, arithmetic and copies ran while one was open for 0% -> 0% of each run, Pallas kernels for 0% -> 0%
where the time goes in v1:
time: 45.8 us; the launch traced here: 45.6 us
  Pallas kernels  43.8 us (96%)
  local copies, waits for them, and re-layouts  1.87 us (4%)
    pallas_call x1, Pallas kernels, body(): pl.pallas_call(functools.partial(kernel, 1.0 / samples), out_shape=jax.Sh...  43.8 us
    unnamed x1, local copies, waits for them, and re-layouts  1.87 us

profile of v1, /device:TPU:1, one launch (start us, length us, event | category | flops | bytes accessed | tf_op | source)
XLA Modules:
  0.0 45.6 jit_solution(16488809235114475763)
XLA Ops:
  0.0 43.8 %shard_map.28 = f32[2,4,8,2048]{3,2,1,0:T(8,128)} custom-call(bf16[512,128]{1,0:T(8,128)(2,1)} %bitcast.2, bf16[2,128,16]{2,1,0:T(8,128)(2,1)} %bitcast.3), custom_call_target="tpu_custom_call" | custom-call | tf_op jit(solution)/shard_map/pallas_call | solution.py:266
  43.8 1.9 %copy.4 = f32[2,4,8,2048]{3,2,1,0:T(8,128)} copy(f32[2,4,8,2048]{3,2,1,0:T(8,128)} %shard_map.28) | data formatting | bytes 1048576

commit v2 on v1

v2 whole, which is shorter than its diff:
```python
import functools

import jax
import jax.numpy as jnp
from jax import lax
from jax.experimental import pallas as pl
from jax.experimental.pallas import tpu as pltpu
from jax.sharding import PartitionSpec as P

MESH = pl.DeviceIdType.MESH
F32, BF16 = jnp.float32, jnp.bfloat16
RING, YS, CORES, PARTS = 8, 2, 2, 4
NB, CH, HALF = 8, 16, 2
FAR = (4, 3, 5, 2, 6, 1, 7)


def iota(shape, dim):
    return lax.broadcasted_iota(jnp.int32, shape, dim)


def beam_matrix(w_ref):
    elems = w_ref.shape[1] // NB
    spread = (iota((CH, elems * CH), 1) % CH == iota((CH, elems * CH), 0)).astype(F32).astype(BF16)
    shape = (NB * elems, elems * CH)
    own = iota(shape, 0) % elems == iota(shape, 1) // CH
    shape = (2 * NB, NB * elems)
    pick = (iota(shape, 0) % NB == iota(shape, 1) // elems).astype(F32).astype(BF16)
    flat = []
    for part in range(2):
        wide = jnp.dot(w_ref[part], spread, preferred_element_type=F32)
        wide = jnp.where(own, wide, 0.0).astype(BF16)
        flat.append(jnp.dot(pick, wide, preferred_element_type=F32))
    top = iota(flat[0].shape, 0) < NB
    left = jnp.where(top, flat[0], -flat[1])
    right = jnp.where(top, flat[1], flat[0])
    both = jnp.concatenate([left, right], axis=1)
    lane = iota(both.shape, 1) % CH
    return jnp.concatenate(
        [jnp.where(lane == c, both, 0.0).astype(BF16) for c in range(CH)], axis=0
    )


def kernel(scale, volt_hbm, w_hbm, ret, volt, w, part32, part16, got, mine, cols, rows, res,
           in_sem, es_sem, er_sem, gs_sem, cr_sem, rr_sem, ts_sem, tr_sem):
    s, e = lax.axis_index("stn"), lax.axis_index("elem")
    k, x = lax.rem(s, 2), lax.rem(s // 2, RING)
    z, y = lax.rem(s // (2 * RING), RING), s // (2 * RING * RING)
    r_own, w_own = x + k * (z - x), z + k * (x - z)

    def at(yy, rr, ww, kk):
        zz, xx = ww + k * (rr - ww), rr + k * (ww - rr)
        return {"stn": ((yy * RING + zz) * RING + xx) * 2 + kk, "elem": e}

    def along_r(dy, d, kk):
        return at(lax.rem(y + dy, YS), lax.rem(r_own + d, RING), w_own, kk)

    def along_w(dy, d, kk):
        return at(lax.rem(y + dy, YS), r_own, lax.rem(w_own + d, RING), kk)

    partner = at(y, r_own, w_own, 1 - k)

    barrier = pltpu.get_barrier_semaphore()
    peers = 0

    def greet(device):
        nonlocal peers
        pl.semaphore_signal(barrier, inc=1, device_id=device, device_id_type=MESH)
        peers += 1

    for d in (2, 1, 3):
        greet({"stn": s, "elem": lax.rem(e + d, PARTS)})
    for d in FAR:
        for dy in (1, 0):
            greet(along_r(dy, d, k))
            greet(along_r(dy, d, 1 - k))
            greet(along_w(dy, d, 1 - k))
        greet(along_w(0, d, k))
    greet(along_r(1, 0, k))
    greet(along_r(1, 0, 1 - k))
    greet(partner)

    load_v = pltpu.make_async_copy(volt_hbm, volt, in_sem.at[0])
    load_w = pltpu.make_async_copy(w_hbm, w, in_sem.at[1])
    load_w.start()
    load_v.start()
    load_w.wait()
    matrix = beam_matrix(w)
    load_v.wait()
    partial = jnp.dot(matrix, volt[...], preferred_element_type=F32)
    part32[...] = partial
    part16[...] = partial.astype(part16.dtype)
    pl.semaphore_wait(barrier, peers)

    quarter = part32.shape[0] // PARTS
    sends = []
    for d in (2, 1, 3):
        q = lax.rem(e + d, PARTS)
        copy = pltpu.make_async_remote_copy(
            src_ref=part16.at[pl.ds(pl.multiple_of(q * quarter, quarter), quarter)],
            dst_ref=got.at[d - 1],
            send_sem=es_sem.at[d - 1],
            recv_sem=er_sem.at[d - 1],
            device_id={"stn": s, "elem": q},
            device_id_type=MESH,
        )
        copy.start()
        sends.append(copy)
    total = part32[pl.ds(pl.multiple_of(e * quarter, quarter), quarter)]
    for copy in sends[::-1]:
        copy.wait_recv()
    for d in (1, 2, 3):
        total = total + got[d - 1].astype(F32)
    mine[...] = total.astype(BF16).reshape(mine.shape)

    count = 0

    def send(src, dst, sem, device):
        nonlocal count
        copy = pltpu.make_async_remote_copy(
            src_ref=src, dst_ref=dst, send_sem=gs_sem.at[count], recv_sem=sem,
            device_id=device, device_id_type=MESH,
        )
        copy.start()
        sends.append(copy)
        count += 1

    col, row = r_own * 2 + k, w_own * 2 + k
    other_col, other_row = w_own * 2 + k, r_own * 2 + k
    own, other = mine.at[k], mine.at[1 - k]
    for d in FAR:
        send(own, cols.at[y, col], cr_sem.at[y, col], along_r(0, d, k))
        send(other, cols.at[y, other_col], cr_sem.at[y, other_col], along_w(0, d, 1 - k))
    for d in FAR:
        send(own, rows.at[row], rr_sem.at[row], along_w(0, d, k))
        send(other, rows.at[other_row], rr_sem.at[other_row], along_r(0, d, 1 - k))
    for d in FAR + (0,):
        send(own, cols.at[y, col], cr_sem.at[y, col], along_r(1, d, k))
        send(other, cols.at[y, other_col], cr_sem.at[y, other_col], along_w(1, d, 1 - k))
    send(other, cols.at[y, other_col], cr_sem.at[y, other_col], partner)
    send(other, rows.at[other_row], rr_sem.at[other_row], partner)
    half = mine[k]
    cols[y, col] = half
    rows[row] = half

    def landed(dst, sem):
        pltpu.make_async_remote_copy(
            src_ref=dst, dst_ref=dst, send_sem=gs_sem.at[0], recv_sem=sem,
            device_id=partner, device_id_type=MESH,
        ).wait_recv()

    def rows_landed():
        landed(rows.at[w_own * 2 + 1 - k], rr_sem.at[w_own * 2 + 1 - k])
        for d in FAR[::-1]:
            for kk in range(2):
                slot = lax.rem(w_own + d, RING) * 2 + kk
                landed(rows.at[slot], rr_sem.at[slot])

    cross = (((1,), (1,)), ((), ()))
    back = 0
    turned = [None] * HALF
    for dy in range(YS):
        yy = lax.rem(y + dy, YS)
        for d in (0,) + FAR[::-1]:
            base = lax.rem(r_own + d, RING) * 2
            for slot in (base + 1 - k,) if (dy, d) == (0, 0) else (base, base + 1):
                landed(cols.at[yy, slot], cr_sem.at[yy, slot])
        if dy == 0:
            rows_landed()
        for c in range(HALF):
            tile = rows[:, c]
            n, _, samples = tile.shape
            if dy == 0:
                wide = tile.astype(F32).reshape(n, 2, NB, samples)
                wide = jnp.concatenate([wide[:, 1:], -wide[:, :1]], axis=1)
                turned[c] = wide.reshape(n * 2 * NB, samples).astype(BF16)
            wide = cols[yy, :, c].astype(F32).reshape(RING * CORES, 2, NB, samples)
            real, imag = (wide[:, p].reshape(RING * CORES * NB, samples).astype(BF16) for p in range(2))
            prod = lax.dot_general(tile.reshape(n * 2 * NB, samples), real, cross, preferred_element_type=F32)
            prod += lax.dot_general(turned[c], imag, cross, preferred_element_type=F32)
            res[yy, :, c] = (prod * scale).astype(BF16).reshape(n, 2 * NB, -1)
        for d in FAR + (0,):
            slot = lax.rem(w_own + d, RING) * 2
            for kk in (1 - k,) if d == 0 else (0, 1):
                copy = pltpu.make_async_remote_copy(
                    src_ref=res.at[yy, slot + kk], dst_ref=ret.at[k, yy, w_own], send_sem=ts_sem.at[back],
                    recv_sem=tr_sem.at[k, yy, w_own], device_id=along_w(0, d, kk), device_id_type=MESH,
                )
                copy.start()
                sends.append(copy)
                back += 1
        ret[k, yy, w_own] = res[yy, row]

    for dy in range(YS):
        yy = lax.rem(y + dy, YS)
        for d in (0,) + FAR[::-1]:
            if d:
                slot = lax.rem(w_own + d, RING)
                landed(ret.at[k, yy, slot], tr_sem.at[k, yy, slot])
            slot = lax.rem(r_own + d, RING)
            landed(ret.at[1 - k, yy, slot], tr_sem.at[1 - k, yy, slot])
    for copy in sends:
        copy.wait_send()


def unpack(ret, out_hbm, out, sem):
    lanes = ret.shape[-1]
    group = iota((2 * NB, lanes), 1) // (CORES * NB)
    copies = []
    for h in range(2):
        for c in range(HALF):
            for yy in range(YS):
                tiles = [ret[h, yy, i, c].astype(F32) for i in range(RING)]
                for bit in (1, 2, 4) if h else ():
                    high = (group // bit) % 2 == 1
                    swapped = list(tiles)
                    for i in range(RING):
                        if i & bit:
                            continue
                        a, b = tiles[i], tiles[i | bit]
                        shift = bit * CORES * NB
                        swapped[i] = jnp.where(high, pltpu.roll(b, shift, 1), a)
                        swapped[i | bit] = jnp.where(high, b, pltpu.roll(a, lanes - shift, 1))
                    tiles = swapped
                for i in range(RING):
                    where = pl.ds((yy * RING + i) * lanes, lanes)
                    for part in range(2):
                        out[part, h * HALF + c, :, where] = tiles[i][part * NB:(part + 1) * NB]
            for part in range(2):
                ch = h * HALF + c
                copy = pltpu.make_async_copy(out.at[part, ch], out_hbm.at[part, ch], sem.at[part, ch])
                copy.start()
                copies.append(copy)
    for copy in copies:
        copy.wait()


def body(voltages, weights):
    samples = voltages.shape[4]
    elems = voltages.shape[2]
    mine_ch = CH // PARTS
    volt = voltages.reshape(2 * elems * CH, samples)
    w = weights.reshape(2, NB * elems, CH)
    lanes = RING * CORES * NB
    block = (HALF, 2 * NB, samples)
    result = (HALF, 2 * NB, lanes)
    gathers = 4 * (RING - 1) + 2 * RING + 2
    dma = pltpu.SemaphoreType.DMA
    ret = pl.pallas_call(
        functools.partial(kernel, 1.0 / samples),
        out_shape=pltpu.VMEM((2, YS, RING) + result, BF16),
        in_specs=[pl.BlockSpec(memory_space=pl.ANY)] * 2,
        out_specs=pl.BlockSpec(memory_space=pltpu.VMEM),
        scratch_shapes=[
            pltpu.VMEM(volt.shape, BF16),
            pltpu.VMEM(w.shape, BF16),
            pltpu.VMEM((CH * 2 * NB, samples), F32),
            pltpu.VMEM((CH * 2 * NB, samples), BF16),
            pltpu.VMEM((PARTS - 1, mine_ch * 2 * NB, samples), BF16),
            pltpu.VMEM((2,) + block, BF16),
            pltpu.VMEM((YS, RING * CORES) + block, BF16),
            pltpu.VMEM((RING * CORES,) + block, BF16),
            pltpu.VMEM((YS, RING * CORES) + result, BF16),
            dma((2,)),
            dma((PARTS - 1,)),
            dma((PARTS - 1,)),
            dma((gathers,)),
            dma((YS, RING * CORES)),
            dma((RING * CORES,)),
            dma((YS * RING * CORES,)),
            dma((2, YS, RING)),
        ],
        compiler_params=pltpu.CompilerParams(collective_id=0, has_side_effects=True),
    )(volt, w)
    shape = (2, mine_ch, NB, YS * RING * lanes)
    return pl.pallas_call(
        unpack,
        out_shape=jax.ShapeDtypeStruct(shape, F32),
        in_specs=[pl.BlockSpec(memory_space=pltpu.VMEM)],
        out_specs=pl.BlockSpec(memory_space=pl.ANY),
        scratch_shapes=[pltpu.VMEM(shape, F32), dma((2, mine_ch))],
    )(pltpu.with_memory_space_constraint(ret, pltpu.VMEM))


def solution(mesh):
    placed = (P(None, "stn", "elem", None, None), P(None, None, "elem", None))
    return jax.shard_map(
        body, mesh=mesh, in_specs=placed, out_specs=P(None, "elem", "stn", None), check_vma=False
    )
```

time: 45.8 us -> 44.6 us (0.974)
  local copies, waits for them, and re-layouts: 1.87 us -> 0 us
  Pallas kernels: 43.8 us -> 44.4 us
    unnamed x1 -> x0, local copies, waits for them, and re-layouts: 1.87 us -> none
    pallas_call x1 -> x2, Pallas kernels: 43.8 us -> 44.4 us  [the longest x1 43.4 us: body(): pl.pallas_call(functools.partial(kernel, 1.0 / samples), out_shape=pltpu....]
where the time goes in v2:
time: 44.6 us; the launch traced here: 44.4 us
  Pallas kernels  44.4 us (100%)
    pallas_call x1, Pallas kernels, body(): pl.pallas_call(functools.partial(kernel, 1.0 / samples), out_shape=pltpu....  43.4 us
    pallas_call x1, Pallas kernels, body(): pl.pallas_call(unpack, out_shape=jax.ShapeDtypeStruct(shape, F32), in_spe...  1 us

profile of v2, /device:TPU:1, one launch (start us, length us, event | category | flops | bytes accessed | tf_op | source)
XLA Modules:
  0.0 44.4 jit_solution(14905296015695220426)
XLA Ops:
  0.0 43.4 %shard_map.28.ret = bf16[2,2,8,2,16,128]{5,4,3,2,1,0:T(8,128)(2,1)S(1)} custom-call(bf16[512,128]{1,0:T(8,128)(2,1)} %bitcast.2, bf16[2,128,16]{2,1,0:T(8,128)(2,1)} %bitcast.3), custom_call_target="tpu_custom_call" | custom-call | tf_op jit(solution)/shard_map/pallas_call | solution.py:248
  43.4 1.0 %shard_map.29 = f32[2,4,8,2048]{3,2,1,0:T(8,128)} custom-call(bf16[2,2,8,2,16,128]{5,4,3,2,1,0:T(8,128)(2,1)S(1)} %shard_map.28.ret), custom_call_target="tpu_custom_call" | custom-call | tf_op jit(solution)/shard_map/pallas_call | solution.py:275

commit v3 on v2

--- a/solution.py
+++ b/solution.py
@@ -40,7 +40,7 @@
     )
 
 
-def kernel(scale, volt_hbm, w_hbm, ret, volt, w, part32, part16, got, mine, cols, rows, res,
+def kernel(scale, volt_hbm, w_hbm, ret, early, volt, w, part32, part16, got, mine, cols, rows, res,
            in_sem, es_sem, er_sem, gs_sem, cr_sem, rr_sem, ts_sem, tr_sem):
     s, e = lax.axis_index("stn"), lax.axis_index("elem")
     k, x = lax.rem(s, 2), lax.rem(s // 2, RING)
@@ -58,6 +58,11 @@
         return at(lax.rem(y + dy, YS), r_own, lax.rem(w_own + d, RING), kk)
 
     partner = at(y, r_own, w_own, 1 - k)
+
+    load_v = pltpu.make_async_copy(volt_hbm, volt, in_sem.at[0])
+    load_w = pltpu.make_async_copy(w_hbm, w, in_sem.at[1])
+    load_w.start()
+    load_v.start()
 
     barrier = pltpu.get_barrier_semaphore()
     peers = 0
@@ -79,10 +84,6 @@
     greet(along_r(1, 0, 1 - k))
     greet(partner)
 
-    load_v = pltpu.make_async_copy(volt_hbm, volt, in_sem.at[0])
-    load_w = pltpu.make_async_copy(w_hbm, w, in_sem.at[1])
-    load_w.start()
-    load_v.start()
     load_w.wait()
     matrix = beam_matrix(w)
     load_v.wait()
@@ -92,25 +93,34 @@
     pl.semaphore_wait(barrier, peers)
 
     quarter = part32.shape[0] // PARTS
-    sends = []
-    for d in (2, 1, 3):
-        q = lax.rem(e + d, PARTS)
-        copy = pltpu.make_async_remote_copy(
-            src_ref=part16.at[pl.ds(pl.multiple_of(q * quarter, quarter), quarter)],
-            dst_ref=got.at[d - 1],
-            send_sem=es_sem.at[d - 1],
-            recv_sem=er_sem.at[d - 1],
-            device_id={"stn": s, "elem": q},
-            device_id_type=MESH,
-        )
-        copy.start()
-        sends.append(copy)
-    total = part32[pl.ds(pl.multiple_of(e * quarter, quarter), quarter)]
-    for copy in sends[::-1]:
-        copy.wait_recv()
-    for d in (1, 2, 3):
-        total = total + got[d - 1].astype(F32)
-    mine[...] = total.astype(BF16).reshape(mine.shape)
+    piece = quarter // 2
+
+    def rows_of(q, h):
+        return pl.ds(pl.multiple_of(q * quarter + h * piece, piece), piece)
+
+    sends, partials = [], ([], [])
+    for turn, h in enumerate((k, 1 - k)):
+        for d in (2, 1, 3):
+            q = lax.rem(e + d, PARTS)
+            copy = pltpu.make_async_remote_copy(
+                src_ref=part16.at[rows_of(q, h)],
+                dst_ref=got.at[d - 1, turn],
+                send_sem=es_sem.at[d - 1, turn],
+                recv_sem=er_sem.at[d - 1, turn],
+                device_id={"stn": s, "elem": q},
+                device_id_type=MESH,
+            )
+            copy.start()
+            sends.append(copy)
+            partials[turn].append(copy)
+
+    def add_up(turn, h):
+        total = part32[rows_of(e, h)]
+        for copy in partials[turn][::-1]:
+            copy.wait_recv()
+        for d in (1, 2, 3):
+            total = total + got[d - 1, turn].astype(F32)
+        mine[h] = total.astype(BF16).reshape(mine.shape[1:])
 
     count = 0
 
@@ -127,15 +137,22 @@
     col, row = r_own * 2 + k, w_own * 2 + k
     other_col, other_row = w_own * 2 + k, r_own * 2 + k
     own, other = mine.at[k], mine.at[1 - k]
+    add_up(0, k)
+    for d in FAR:
+        send(own, cols.at[y, col], cr_sem.at[y, col], along_r(1, d, k))
+    for d in FAR:
+        send(own, rows.at[row], rr_sem.at[row], along_w(0, d, k))
     for d in FAR:
         send(own, cols.at[y, col], cr_sem.at[y, col], along_r(0, d, k))
+    send(own, cols.at[y, col], cr_sem.at[y, col], along_r(1, 0, k))
+    add_up(1, 1 - k)
+    for d in FAR:
+        send(other, cols.at[y, other_col], cr_sem.at[y, other_col], along_w(1, d, 1 - k))
+    for d in FAR:
+        send(other, rows.at[other_row], rr_sem.at[other_row], along_r(0, d, 1 - k))
+    for d in FAR:
         send(other, cols.at[y, other_col], cr_sem.at[y, other_col], along_w(0, d, 1 - k))
-    for d in FAR:
-        send(own, rows.at[row], rr_sem.at[row], along_w(0, d, k))
-        send(other, rows.at[other_row], rr_sem.at[other_row], along_r(0, d, 1 - k))
-    for d in FAR + (0,):
-        send(own, cols.at[y, col], cr_sem.at[y, col], along_r(1, d, k))
-        send(other, cols.at[y, other_col], cr_sem.at[y, other_col], along_w(1, d, 1 - k))
+    send(other, cols.at[y, other_col], cr_sem.at[y, other_col], along_w(1, 0, 1 - k))
     send(other, cols.at[y, other_col], cr_sem.at[y, other_col], partner)
     send(other, rows.at[other_row], rr_sem.at[other_row], partner)
     half = mine[k]
@@ -158,18 +175,18 @@
     cross = (((1,), (1,)), ((), ()))
     back = 0
     turned = [None] * HALF
-    for dy in range(YS):
+    for dy in (1, 0):
         yy = lax.rem(y + dy, YS)
         for d in (0,) + FAR[::-1]:
             base = lax.rem(r_own + d, RING) * 2
             for slot in (base + 1 - k,) if (dy, d) == (0, 0) else (base, base + 1):
                 landed(cols.at[yy, slot], cr_sem.at[yy, slot])
-        if dy == 0:
+        if dy == 1:
             rows_landed()
         for c in range(HALF):
             tile = rows[:, c]
             n, _, samples = tile.shape
-            if dy == 0:
+            if dy == 1:
                 wide = tile.astype(F32).reshape(n, 2, NB, samples)
                 wide = jnp.concatenate([wide[:, 1:], -wide[:, :1]], axis=1)
                 turned[c] = wide.reshape(n * 2 * NB, samples).astype(BF16)
@@ -190,7 +207,10 @@
                 back += 1
         ret[k, yy, w_own] = res[yy, row]
 
-    for dy in range(YS):
+    for copy in sends:
+        copy.wait_send()
+
+    for dy in (1, 0):
         yy = lax.rem(y + dy, YS)
         for d in (0,) + FAR[::-1]:
             if d:
@@ -198,40 +218,46 @@
                 landed(ret.at[k, yy, slot], tr_sem.at[k, yy, slot])
             slot = lax.rem(r_own + d, RING)
             landed(ret.at[1 - k, yy, slot], tr_sem.at[1 - k, yy, slot])
-    for copy in sends:
-        copy.wait_send()
-
-
-def unpack(ret, out_hbm, out, sem):
+        if dy == 1:
+            unpack(ret, early, yy)
+
+
+def unpack(ret, out, yy):
     lanes = ret.shape[-1]
     group = iota((2 * NB, lanes), 1) // (CORES * NB)
-    copies = []
     for h in range(2):
         for c in range(HALF):
-            for yy in range(YS):
-                tiles = [ret[h, yy, i, c].astype(F32) for i in range(RING)]
-                for bit in (1, 2, 4) if h else ():
-                    high = (group // bit) % 2 == 1
-                    swapped = list(tiles)
-                    for i in range(RING):
-                        if i & bit:
-                            continue
-                        a, b = tiles[i], tiles[i | bit]
-                        shift = bit * CORES * NB
-                        swapped[i] = jnp.where(high, pltpu.roll(b, shift, 1), a)
-                        swapped[i | bit] = jnp.where(high, b, pltpu.roll(a, lanes - shift, 1))
-                    tiles = swapped
+            tiles = [ret[h, yy, i, c].astype(F32) for i in range(RING)]
+            for bit in (1, 2, 4) if h else ():
+                high = (group // bit) % 2 == 1
+                swapped = list(tiles)
                 for i in range(RING):
-                    where = pl.ds((yy * RING + i) * lanes, lanes)
-                    for part in range(2):
-                        out[part, h * HALF + c, :, where] = tiles[i][part * NB:(part + 1) * NB]
-            for part in range(2):
-                ch = h * HALF + c
-                copy = pltpu.make_async_copy(out.at[part, ch], out_hbm.at[part, ch], sem.at[part, ch])
-                copy.start()
-                copies.append(copy)
-    for copy in copies:
-        copy.wait()
+                    if i & bit:
+                        continue
+                    a, b = tiles[i], tiles[i | bit]
+                    shift = bit * CORES * NB
+                    swapped[i] = jnp.where(high, pltpu.roll(b, shift, 1), a)
+                    swapped[i | bit] = jnp.where(high, b, pltpu.roll(a, lanes - shift, 1))
+                tiles = swapped
+            for i in range(RING):
+                for part in range(2):
+                    out[part, h * HALF + c, :, pl.ds(i * lanes, lanes)] = tiles[i][part * NB:(part + 1) * NB]
+
+
+def place(out_hbm, yy):
+    width = out_hbm.shape[3] // YS
+    return out_hbm.at[:, :, :, pl.ds(pl.multiple_of(yy * width, width), width)]
+
+
+def finish(ret, early, out_hbm, out, sem):
+    y = lax.axis_index("stn") // (2 * RING * RING)
+    first = pltpu.make_async_copy(early, place(out_hbm, 1 - y), sem.at[0])
+    first.start()
+    unpack(ret, out, y)
+    last = pltpu.make_async_copy(out, place(out_hbm, y), sem.at[1])
+    last.start()
+    first.wait()
+    last.wait()
 
 
 def body(voltages, weights):
@@ -245,24 +271,26 @@
     result = (HALF, 2 * NB, lanes)
     gathers = 4 * (RING - 1) + 2 * RING + 2
     dma = pltpu.SemaphoreType.DMA
-    ret = pl.pallas_call(
+    shape = (2, mine_ch, NB, YS * RING * lanes)
+    half = shape[:3] + (RING * lanes,)
+    ret, early = pl.pallas_call(
         functools.partial(kernel, 1.0 / samples),
-        out_shape=pltpu.VMEM((2, YS, RING) + result, BF16),
+        out_shape=(pltpu.VMEM((2, YS, RING) + result, BF16), pltpu.VMEM(half, F32)),
         in_specs=[pl.BlockSpec(memory_space=pl.ANY)] * 2,
-        out_specs=pl.BlockSpec(memory_space=pltpu.VMEM),
+        out_specs=(pl.BlockSpec(memory_space=pltpu.VMEM),) * 2,
         scratch_shapes=[
             pltpu.VMEM(volt.shape, BF16),
             pltpu.VMEM(w.shape, BF16),
             pltpu.VMEM((CH * 2 * NB, samples), F32),
             pltpu.VMEM((CH * 2 * NB, samples), BF16),
-            pltpu.VMEM((PARTS - 1, mine_ch * 2 * NB, samples), BF16),
+            pltpu.VMEM((PARTS - 1, 2, HALF * 2 * NB, samples), BF16),
             pltpu.VMEM((2,) + block, BF16),
             pltpu.VMEM((YS, RING * CORES) + block, BF16),
             pltpu.VMEM((RING * CORES,) + block, BF16),
             pltpu.VMEM((YS, RING * CORES) + result, BF16),
             dma((2,)),
-            dma((PARTS - 1,)),
-            dma((PARTS - 1,)),
+            dma((PARTS - 1, 2)),
+            dma((PARTS - 1, 2)),
             dma((gathers,)),
             dma((YS, RING * CORES)),
             dma((RING * CORES,)),
@@ -271,14 +299,13 @@
         ],
         compiler_params=pltpu.CompilerParams(collective_id=0, has_side_effects=True),
     )(volt, w)
-    shape = (2, mine_ch, NB, YS * RING * lanes)
     return pl.pallas_call(
-        unpack,
+        finish,
         out_shape=jax.ShapeDtypeStruct(shape, F32),
-        in_specs=[pl.BlockSpec(memory_space=pltpu.VMEM)],
+        in_specs=[pl.BlockSpec(memory_space=pltpu.VMEM)] * 2,
         out_specs=pl.BlockSpec(memory_space=pl.ANY),
-        scratch_shapes=[pltpu.VMEM(shape, F32), dma((2, mine_ch))],
-    )(pltpu.with_memory_space_constraint(ret, pltpu.VMEM))
+        scratch_shapes=[pltpu.VMEM(half, F32), dma((2,))],
+    )(*(pltpu.with_memory_space_constraint(a, pltpu.VMEM) for a in (ret, early)))
 
 
 def solution(mesh):

time: 44.6 us -> 43.3 us (0.971)
  Pallas kernels: 44.4 us -> 43.1 us
    pallas_call x2, Pallas kernels: 44.4 us -> 43.1 us  [the longest x1 42.2 us: body(): pl.pallas_call(functools.partial(kernel, 1.0 / samples), out_shape=(pltpu...]
where the time goes in v3:
time: 43.3 us; the launch traced here: 43.1 us
  Pallas kernels  43.1 us (100%)
    pallas_call x1, Pallas kernels, body(): pl.pallas_call(functools.partial(kernel, 1.0 / samples), out_shape=(pltpu...  42.2 us
    pallas_call x1, Pallas kernels, body(): pl.pallas_call(finish, out_shape=jax.ShapeDtypeStruct(shape, F32), in_spe...  0.97 us

profile of v3, /device:TPU:1, one launch (start us, length us, event | category | flops | bytes accessed | tf_op | source)
XLA Modules:
  0.0 43.1 jit_solution(8959080279188231772)
XLA Ops:
  0.0 42.2 %shard_map.28 = (bf16[2,2,8,2,16,128]{5,4,3,2,1,0:T(8,128)(2,1)S(1)}, f32[2,4,8,1024]{3,2,1,0:T(8,128)S(1)}) custom-call(bf16[512,128]{1,0:T(8,128)(2,1)} %bitcast.2, bf16[2,128,16]{2,1,0:T(8,128)(2,1)} %bitcast.3), custom_call_target="tpu_custom_call" | custom-call | tf_op jit(solution)/shard_map/pallas_call | solution.py:276
  42.2 1.0 %shard_map.29 = f32[2,4,8,2048]{3,2,1,0:T(8,128)} custom-call(bf16[2,2,8,2,16,128]{5,4,3,2,1,0:T(8,128)(2,1)S(1)} %get-tuple-element.7.ret, f32[2,4,8,1024]{3,2,1,0:T(8,128)S(1)} %get-tuple-element.8.early), custom_call_target="tpu_custom_call" | custom-call | tf_op jit(solution)/shard_map/pallas_call | solution.py:302

commit v4 on v3

--- a/solution.py
+++ b/solution.py
@@ -41,7 +41,7 @@
 
 
 def kernel(scale, volt_hbm, w_hbm, ret, early, volt, w, part32, part16, got, mine, cols, rows, res,
-           in_sem, es_sem, er_sem, gs_sem, cr_sem, rr_sem, ts_sem, tr_sem):
+           in_sem, es_sem, er_sem, gs_sem, cr_sem, rr_sem, ts_sem, tr_sem, here, zs_sem):
     s, e = lax.axis_index("stn"), lax.axis_index("elem")
     k, x = lax.rem(s, 2), lax.rem(s // 2, RING)
     z, y = lax.rem(s // (2 * RING), RING), s // (2 * RING * RING)
@@ -58,31 +58,36 @@
         return at(lax.rem(y + dy, YS), r_own, lax.rem(w_own + d, RING), kk)
 
     partner = at(y, r_own, w_own, 1 - k)
+    facing = at(1 - y, r_own, w_own, k)
 
     load_v = pltpu.make_async_copy(volt_hbm, volt, in_sem.at[0])
     load_w = pltpu.make_async_copy(w_hbm, w, in_sem.at[1])
     load_w.start()
     load_v.start()
 
+    def device(zz, xx, kk):
+        return {"stn": ((y * RING + zz) * RING + xx) * 2 + kk, "elem": e}
+
     barrier = pltpu.get_barrier_semaphore()
     peers = 0
 
-    def greet(device):
+    def greet(peer):
         nonlocal peers
-        pl.semaphore_signal(barrier, inc=1, device_id=device, device_id_type=MESH)
+        pl.semaphore_signal(barrier, inc=1, device_id=peer, device_id_type=MESH)
         peers += 1
 
     for d in (2, 1, 3):
         greet({"stn": s, "elem": lax.rem(e + d, PARTS)})
     for d in FAR:
-        for dy in (1, 0):
-            greet(along_r(dy, d, k))
-            greet(along_r(dy, d, 1 - k))
-            greet(along_w(dy, d, 1 - k))
-        greet(along_w(0, d, k))
-    greet(along_r(1, 0, k))
-    greet(along_r(1, 0, 1 - k))
+        for kk in range(CORES):
+            greet(device(z, lax.rem(x + d, RING), kk))
+    greet(facing)
     greet(partner)
+    for zz in range(1, RING):
+        @pl.when(zz > z)
+        def _():
+            for kk in range(CORES):
+                pl.semaphore_signal(barrier, inc=1, device_id=device(zz, x, kk), device_id_type=MESH)
 
     load_w.wait()
     matrix = beam_matrix(w)
@@ -90,7 +95,12 @@
     partial = jnp.dot(matrix, volt[...], preferred_element_type=F32)
     part32[...] = partial
     part16[...] = partial.astype(part16.dtype)
-    pl.semaphore_wait(barrier, peers)
+    pl.semaphore_wait(barrier, peers + CORES * z)
+    for zz in range(RING - 1):
+        @pl.when(zz < z)
+        def _():
+            for kk in range(CORES):
+                pl.semaphore_signal(here.at[z], inc=1, device_id=device(zz, x, kk), device_id_type=MESH)
 
     quarter = part32.shape[0] // PARTS
     piece = quarter // 2
@@ -136,25 +146,37 @@
 
     col, row = r_own * 2 + k, w_own * 2 + k
     other_col, other_row = w_own * 2 + k, r_own * 2 + k
-    own, other = mine.at[k], mine.at[1 - k]
     add_up(0, k)
-    for d in FAR:
-        send(own, cols.at[y, col], cr_sem.at[y, col], along_r(1, d, k))
-    for d in FAR:
-        send(own, rows.at[row], rr_sem.at[row], along_w(0, d, k))
-    for d in FAR:
-        send(own, cols.at[y, col], cr_sem.at[y, col], along_r(0, d, k))
-    send(own, cols.at[y, col], cr_sem.at[y, col], along_r(1, 0, k))
     add_up(1, 1 - k)
     for d in FAR:
-        send(other, cols.at[y, other_col], cr_sem.at[y, other_col], along_w(1, d, 1 - k))
+        xx = lax.rem(x + d, RING)
+        send(mine.at[0], cols.at[y, x * 2 + k], cr_sem.at[y, x * 2 + k], device(z, xx, 0))
     for d in FAR:
-        send(other, rows.at[other_row], rr_sem.at[other_row], along_r(0, d, 1 - k))
-    for d in FAR:
-        send(other, cols.at[y, other_col], cr_sem.at[y, other_col], along_w(0, d, 1 - k))
-    send(other, cols.at[y, other_col], cr_sem.at[y, other_col], along_w(1, 0, 1 - k))
+        xx = lax.rem(x + d, RING)
+        send(mine.at[1], rows.at[x * 2 + k], rr_sem.at[x * 2 + k], device(z, xx, 1))
+    other = mine.at[1 - k]
     send(other, cols.at[y, other_col], cr_sem.at[y, other_col], partner)
     send(other, rows.at[other_row], rr_sem.at[other_row], partner)
+
+    def to_plane(zz):
+        slot = z * 2 + k
+        return [
+            pltpu.make_async_remote_copy(
+                src_ref=mine.at[1 - h], dst_ref=dst, send_sem=zs_sem.at[zz, h], recv_sem=sem,
+                device_id=device(zz, x, 1 - h), device_id_type=MESH,
+            )
+            for h, (dst, sem) in enumerate(((cols.at[y, slot], cr_sem.at[y, slot]), (rows.at[slot], rr_sem.at[slot])))
+        ]
+
+    for zz in range(RING):
+        @pl.when(zz > z)
+        def _():
+            pl.semaphore_wait(here.at[zz], CORES)
+
+        @pl.when(zz != z)
+        def _():
+            for copy in to_plane(zz):
+                copy.start()
     half = mine[k]
     cols[y, col] = half
     rows[row] = half
@@ -175,18 +197,30 @@
     cross = (((1,), (1,)), ((), ()))
     back = 0
     turned = [None] * HALF
-    for dy in (1, 0):
+    for rr in range(RING):
+        base = rr * 2
+
+        @pl.when(rr != r_own)
+        def _():
+            for slot in (base, base + 1):
+                landed(cols.at[y, slot], cr_sem.at[y, slot])
+
+        @pl.when(rr == r_own)
+        def _():
+            landed(cols.at[y, base + 1 - k], cr_sem.at[y, base + 1 - k])
+
+        pair = cols.at[y, pl.ds(base, 2)]
+        send(pair, pair, cr_sem.at[y, base], facing)
+    rows_landed()
+    for dy in range(YS):
         yy = lax.rem(y + dy, YS)
-        for d in (0,) + FAR[::-1]:
-            base = lax.rem(r_own + d, RING) * 2
-            for slot in (base + 1 - k,) if (dy, d) == (0, 0) else (base, base + 1):
-                landed(cols.at[yy, slot], cr_sem.at[yy, slot])
         if dy == 1:
-            rows_landed()
+            for base in range(0, 2 * RING, 2):
+                landed(cols.at[yy, pl.ds(base, 2)], cr_sem.at[yy, base])
         for c in range(HALF):
             tile = rows[:, c]
             n, _, samples = tile.shape
-            if dy == 1:
+            if dy == 0:
                 wide = tile.astype(F32).reshape(n, 2, NB, samples)
                 wide = jnp.concatenate([wide[:, 1:], -wide[:, :1]], axis=1)
                 turned[c] = wide.reshape(n * 2 * NB, samples).astype(BF16)
@@ -209,8 +243,13 @@
 
     for copy in sends:
         copy.wait_send()
-
-    for dy in (1, 0):
+    for zz in range(RING):
+        @pl.when(zz != z)
+        def _():
+            for copy in to_plane(zz):
+                copy.wait_send()
+
+    for dy in range(YS):
         yy = lax.rem(y + dy, YS)
         for d in (0,) + FAR[::-1]:
             if d:
@@ -218,7 +257,7 @@
                 landed(ret.at[k, yy, slot], tr_sem.at[k, yy, slot])
             slot = lax.rem(r_own + d, RING)
             landed(ret.at[1 - k, yy, slot], tr_sem.at[1 - k, yy, slot])
-        if dy == 1:
+        if dy == 0:
             unpack(ret, early, yy)
 
 
@@ -251,10 +290,10 @@
 
 def finish(ret, early, out_hbm, out, sem):
     y = lax.axis_index("stn") // (2 * RING * RING)
-    first = pltpu.make_async_copy(early, place(out_hbm, 1 - y), sem.at[0])
+    first = pltpu.make_async_copy(early, place(out_hbm, y), sem.at[0])
     first.start()
-    unpack(ret, out, y)
-    last = pltpu.make_async_copy(out, place(out_hbm, y), sem.at[1])
+    unpack(ret, out, 1 - y)
+    last = pltpu.make_async_copy(out, place(out_hbm, 1 - y), sem.at[1])
     last.start()
     first.wait()
     last.wait()
@@ -269,7 +308,7 @@
     lanes = RING * CORES * NB
     block = (HALF, 2 * NB, samples)
     result = (HALF, 2 * NB, lanes)
-    gathers = 4 * (RING - 1) + 2 * RING + 2
+    gathers = 2 * (RING - 1) + RING + 2
     dma = pltpu.SemaphoreType.DMA
     shape = (2, mine_ch, NB, YS * RING * lanes)
     half = shape[:3] + (RING * lanes,)
@@ -296,6 +335,8 @@
             dma((RING * CORES,)),
             dma((YS * RING * CORES,)),
             dma((2, YS, RING)),
+            pltpu.SemaphoreType.REGULAR((RING,)),
+            dma((RING, 2)),
         ],
         compiler_params=pltpu.CompilerParams(collective_id=0, has_side_effects=True),
     )(volt, w)

time: 43.3 us -> 42.9 us (level)
  no operation moved by 1% of the time
where the time goes in v4:
time: 42.9 us; the launch traced here: 42.7 us
  Pallas kernels  42.7 us (100%)
    pallas_call x1, Pallas kernels, body(): pl.pallas_call(functools.partial(kernel, 1.0 / samples), out_shape=(pltpu...  41.8 us
    pallas_call x1, Pallas kernels, body(): pl.pallas_call(finish, out_shape=jax.ShapeDtypeStruct(shape, F32), in_spe...  0.97 us

profile of v4, /device:TPU:1, one launch (start us, length us, event | category | flops | bytes accessed | tf_op | source)
XLA Modules:
  0.0 42.7 jit_solution(393445324603845263)
XLA Ops:
  0.0 41.8 %shard_map.28 = (bf16[2,2,8,2,16,128]{5,4,3,2,1,0:T(8,128)(2,1)S(1)}, f32[2,4,8,1024]{3,2,1,0:T(8,128)S(1)}) custom-call(bf16[512,128]{1,0:T(8,128)(2,1)} %bitcast.2, bf16[2,128,16]{2,1,0:T(8,128)(2,1)} %bitcast.3), custom_call_target="tpu_custom_call" | custom-call | tf_op jit(solution)/shard_map/pallas_call | solution.py:315
  41.8 1.0 %shard_map.29 = f32[2,4,8,2048]{3,2,1,0:T(8,128)} custom-call(bf16[2,2,8,2,16,128]{5,4,3,2,1,0:T(8,128)(2,1)S(1)} %get-tuple-element.7.ret, f32[2,4,8,1024]{3,2,1,0:T(8,128)S(1)} %get-tuple-element.8.early), custom_call_target="tpu_custom_call" | custom-call | tf_op jit(solution)/shard_map/pallas_call | solution.py:343

commit v5 on v4

--- a/solution.py
+++ b/solution.py
@@ -12,6 +12,7 @@
 RING, YS, CORES, PARTS = 8, 2, 2, 4
 NB, CH, HALF = 8, 16, 2
 FAR = (4, 3, 5, 2, 6, 1, 7)
+ORDER = tuple((xx, i) for i, xx in enumerate((0, 1, 7, 2, 6, 3, 5, 4)))
 
 
 def iota(shape, dim):
@@ -41,7 +42,7 @@
 
 
 def kernel(scale, volt_hbm, w_hbm, ret, early, volt, w, part32, part16, got, mine, cols, rows, res,
-           in_sem, es_sem, er_sem, gs_sem, cr_sem, rr_sem, ts_sem, tr_sem, here, zs_sem):
+           in_sem, es_sem, er_sem, gs_sem, cr_sem, rr_sem, ts_sem, tr_sem, here, zs_sem, near, xs_sem):
     s, e = lax.axis_index("stn"), lax.axis_index("elem")
     k, x = lax.rem(s, 2), lax.rem(s // 2, RING)
     z, y = lax.rem(s // (2 * RING), RING), s // (2 * RING * RING)
@@ -68,6 +69,7 @@
     def device(zz, xx, kk):
         return {"stn": ((y * RING + zz) * RING + xx) * 2 + kk, "elem": e}
 
+    my_place = jnp.where(x <= RING // 2, jnp.maximum(2 * x - 1, 0), 2 * (RING - x))
     barrier = pltpu.get_barrier_semaphore()
     peers = 0
 
@@ -78,9 +80,11 @@
 
     for d in (2, 1, 3):
         greet({"stn": s, "elem": lax.rem(e + d, PARTS)})
-    for d in FAR:
-        for kk in range(CORES):
-            greet(device(z, lax.rem(x + d, RING), kk))
+    for xx, place_of in ORDER:
+        @pl.when(place_of > my_place)
+        def _():
+            for kk in range(CORES):
+                pl.semaphore_signal(barrier, inc=1, device_id=device(z, xx, kk), device_id_type=MESH)
     greet(facing)
     greet(partner)
     for zz in range(1, RING):
@@ -95,7 +99,12 @@
     partial = jnp.dot(matrix, volt[...], preferred_element_type=F32)
     part32[...] = partial
     part16[...] = partial.astype(part16.dtype)
-    pl.semaphore_wait(barrier, peers + CORES * z)
+    pl.semaphore_wait(barrier, peers + CORES * (z + my_place))
+    for xx, place_of in ORDER:
+        @pl.when(place_of < my_place)
+        def _():
+            for kk in range(CORES):
+                pl.semaphore_signal(near.at[x], inc=1, device_id=device(z, xx, kk), device_id_type=MESH)
     for zz in range(RING - 1):
         @pl.when(zz < z)
         def _():
@@ -109,7 +118,7 @@
         return pl.ds(pl.multiple_of(q * quarter + h * piece, piece), piece)
 
     sends, partials = [], ([], [])
-    for turn, h in enumerate((k, 1 - k)):
+    for turn, h in enumerate((0, 1)):
         for d in (2, 1, 3):
             q = lax.rem(e + d, PARTS)
             copy = pltpu.make_async_remote_copy(
@@ -146,14 +155,29 @@
 
     col, row = r_own * 2 + k, w_own * 2 + k
     other_col, other_row = w_own * 2 + k, r_own * 2 + k
-    add_up(0, k)
-    add_up(1, 1 - k)
-    for d in FAR:
-        xx = lax.rem(x + d, RING)
-        send(mine.at[0], cols.at[y, x * 2 + k], cr_sem.at[y, x * 2 + k], device(z, xx, 0))
-    for d in FAR:
-        xx = lax.rem(x + d, RING)
-        send(mine.at[1], rows.at[x * 2 + k], rr_sem.at[x * 2 + k], device(z, xx, 1))
+    add_up(0, 0)
+
+    def in_plane(xx, h):
+        slot = x * 2 + k
+        dst, sem = (rows.at[slot], rr_sem.at[slot]) if h else (cols.at[y, slot], cr_sem.at[y, slot])
+        return pltpu.make_async_remote_copy(
+            src_ref=mine.at[h], dst_ref=dst, send_sem=xs_sem.at[xx, h], recv_sem=sem,
+            device_id=device(z, xx, h), device_id_type=MESH,
+        )
+
+    for xx, place_of in ORDER:
+        @pl.when(place_of > my_place)
+        def _():
+            pl.semaphore_wait(near.at[xx], CORES)
+
+        @pl.when(xx != x)
+        def _():
+            in_plane(xx, 0).start()
+    add_up(1, 1)
+    for xx in range(RING):
+        @pl.when(xx != x)
+        def _():
+            in_plane(xx, 1).start()
     other = mine.at[1 - k]
     send(other, cols.at[y, other_col], cr_sem.at[y, other_col], partner)
     send(other, rows.at[other_row], rr_sem.at[other_row], partner)
@@ -197,7 +221,9 @@
     cross = (((1,), (1,)), ((), ()))
     back = 0
     turned = [None] * HALF
-    for rr in range(RING):
+    for i, d in enumerate((0,) + FAR[::-1]):
+        rr = lax.rem(x + d, RING)
+        rr = rr + k * (i - rr)
         base = rr * 2
 
         @pl.when(rr != r_own)
@@ -229,7 +255,7 @@
             prod = lax.dot_general(tile.reshape(n * 2 * NB, samples), real, cross, preferred_element_type=F32)
             prod += lax.dot_general(turned[c], imag, cross, preferred_element_type=F32)
             res[yy, :, c] = (prod * scale).astype(BF16).reshape(n, 2 * NB, -1)
-        for d in FAR + (0,):
+        for d in tuple(range(1, RING)) + (0,):
             slot = lax.rem(w_own + d, RING) * 2
             for kk in (1 - k,) if d == 0 else (0, 1):
                 copy = pltpu.make_async_remote_copy(
@@ -243,11 +269,16 @@
 
     for copy in sends:
         copy.wait_send()
-    for zz in range(RING):
-        @pl.when(zz != z)
-        def _():
-            for copy in to_plane(zz):
+    for i in range(RING):
+        @pl.when(i != z)
+        def _():
+            for copy in to_plane(i):
                 copy.wait_send()
+
+        @pl.when(i != x)
+        def _():
+            for h in range(2):
+                in_plane(i, h).wait_send()
 
     for dy in range(YS):
         yy = lax.rem(y + dy, YS)
@@ -308,7 +339,7 @@
     lanes = RING * CORES * NB
     block = (HALF, 2 * NB, samples)
     result = (HALF, 2 * NB, lanes)
-    gathers = 2 * (RING - 1) + RING + 2
+    gathers = RING + 2
     dma = pltpu.SemaphoreType.DMA
     shape = (2, mine_ch, NB, YS * RING * lanes)
     half = shape[:3] + (RING * lanes,)
@@ -337,6 +368,8 @@
             dma((2, YS, RING)),
             pltpu.SemaphoreType.REGULAR((RING,)),
             dma((RING, 2)),
+            pltpu.SemaphoreType.REGULAR((RING,)),
+            dma((RING, 2)),
         ],
         compiler_params=pltpu.CompilerParams(collective_id=0, has_side_effects=True),
     )(volt, w)

time: 42.9 us -> 41.6 us (0.970)
  Pallas kernels: 42.7 us -> 41.4 us
    pallas_call x1, Pallas kernels: 41.8 us -> 40.5 us  [body(): pl.pallas_call(functools.partial(kernel, 1.0 / samples), out_shape=(pltpu...]
where the time goes in v5:
time: 41.6 us; the launch traced here: 41.4 us
  Pallas kernels  41.4 us (100%)
    pallas_call x1, Pallas kernels, body(): pl.pallas_call(functools.partial(kernel, 1.0 / samples), out_shape=(pltpu...  40.5 us
    pallas_call x1, Pallas kernels, body(): pl.pallas_call(finish, out_shape=jax.ShapeDtypeStruct(shape, F32), in_spe...  0.97 us

profile of v5, /device:TPU:1, one launch (start us, length us, event | category | flops | bytes accessed | tf_op | source)
XLA Modules:
  0.0 41.4 jit_solution(18435947307412837142)
XLA Ops:
  0.0 40.5 %shard_map.28 = (bf16[2,2,8,2,16,128]{5,4,3,2,1,0:T(8,128)(2,1)S(1)}, f32[2,4,8,1024]{3,2,1,0:T(8,128)S(1)}) custom-call(bf16[512,128]{1,0:T(8,128)(2,1)} %bitcast.2, bf16[2,128,16]{2,1,0:T(8,128)(2,1)} %bitcast.3), custom_call_target="tpu_custom_call" | custom-call | tf_op jit(solution)/shard_map/pallas_call | solution.py:346
  40.5 1.0 %shard_map.29 = f32[2,4,8,2048]{3,2,1,0:T(8,128)} custom-call(bf16[2,2,8,2,16,128]{5,4,3,2,1,0:T(8,128)(2,1)S(1)} %get-tuple-element.7.ret, f32[2,4,8,1024]{3,2,1,0:T(8,128)S(1)} %get-tuple-element.8.early), custom_call_target="tpu_custom_call" | custom-call | tf_op jit(solution)/shard_map/pallas_call | solution.py:376

commit v6 on v5

--- a/solution.py
+++ b/solution.py
@@ -211,16 +211,7 @@
             device_id=partner, device_id_type=MESH,
         ).wait_recv()
 
-    def rows_landed():
-        landed(rows.at[w_own * 2 + 1 - k], rr_sem.at[w_own * 2 + 1 - k])
-        for d in FAR[::-1]:
-            for kk in range(2):
-                slot = lax.rem(w_own + d, RING) * 2 + kk
-                landed(rows.at[slot], rr_sem.at[slot])
-
     cross = (((1,), (1,)), ((), ()))
-    back = 0
-    turned = [None] * HALF
     for i, d in enumerate((0,) + FAR[::-1]):
         rr = lax.rem(x + d, RING)
         rr = rr + k * (i - rr)
@@ -237,35 +228,53 @@
 
         pair = cols.at[y, pl.ds(base, 2)]
         send(pair, pair, cr_sem.at[y, base], facing)
-    rows_landed()
-    for dy in range(YS):
+    def back(dy, pos, kk):
         yy = lax.rem(y + dy, YS)
-        if dy == 1:
-            for base in range(0, 2 * RING, 2):
-                landed(cols.at[yy, pl.ds(base, 2)], cr_sem.at[yy, base])
-        for c in range(HALF):
-            tile = rows[:, c]
-            n, _, samples = tile.shape
-            if dy == 0:
+        return pltpu.make_async_remote_copy(
+            src_ref=res.at[yy, pos * 2 + kk], dst_ref=ret.at[k, yy, w_own],
+            send_sem=ts_sem.at[(dy * RING + pos) * 2 + kk], recv_sem=tr_sem.at[k, yy, w_own],
+            device_id=at(y, r_own, pos, kk), device_id_type=MESH,
+        )
+
+    for low in (True, False):
+        positions = range(RING // 2) if low else range(RING // 2, RING)
+        first = positions[0] * 2
+        for pos in positions:
+            @pl.when(pos != w_own)
+            def _():
+                for slot in (pos * 2, pos * 2 + 1):
+                    landed(rows.at[slot], rr_sem.at[slot])
+
+            @pl.when(pos == w_own)
+            def _():
+                landed(rows.at[pos * 2 + 1 - k], rr_sem.at[pos * 2 + 1 - k])
+        for dy in range(YS):
+            yy = lax.rem(y + dy, YS)
+            if low and dy == 1:
+                for base in range(0, 2 * RING, 2):
+                    landed(cols.at[yy, pl.ds(base, 2)], cr_sem.at[yy, base])
+            part = slice(first, first + RING)
+            for c in range(HALF):
+                tile = rows[part, c]
+                n, _, samples = tile.shape
                 wide = tile.astype(F32).reshape(n, 2, NB, samples)
                 wide = jnp.concatenate([wide[:, 1:], -wide[:, :1]], axis=1)
-                turned[c] = wide.reshape(n * 2 * NB, samples).astype(BF16)
-            wide = cols[yy, :, c].astype(F32).reshape(RING * CORES, 2, NB, samples)
-            real, imag = (wide[:, p].reshape(RING * CORES * NB, samples).astype(BF16) for p in range(2))
-            prod = lax.dot_general(tile.reshape(n * 2 * NB, samples), real, cross, preferred_element_type=F32)
-            prod += lax.dot_general(turned[c], imag, cross, preferred_element_type=F32)
-            res[yy, :, c] = (prod * scale).astype(BF16).reshape(n, 2 * NB, -1)
-        for d in tuple(range(1, RING)) + (0,):
-            slot = lax.rem(w_own + d, RING) * 2
-            for kk in (1 - k,) if d == 0 else (0, 1):
-                copy = pltpu.make_async_remote_copy(
-                    src_ref=res.at[yy, slot + kk], dst_ref=ret.at[k, yy, w_own], send_sem=ts_sem.at[back],
-                    recv_sem=tr_sem.at[k, yy, w_own], device_id=along_w(0, d, kk), device_id_type=MESH,
-                )
-                copy.start()
-                sends.append(copy)
-                back += 1
-        ret[k, yy, w_own] = res[yy, row]
+                turned = wide.reshape(n * 2 * NB, samples).astype(BF16)
+                wide = cols[yy, :, c].astype(F32).reshape(RING * CORES, 2, NB, samples)
+                real, imag = (wide[:, p].reshape(RING * CORES * NB, samples).astype(BF16) for p in range(2))
+                prod = lax.dot_general(tile.reshape(n * 2 * NB, samples), real, cross, preferred_element_type=F32)
+                prod += lax.dot_general(turned, imag, cross, preferred_element_type=F32)
+                res[yy, part, c] = (prod * scale).astype(BF16).reshape(n, 2 * NB, -1)
+            for pos in positions:
+                @pl.when(pos != w_own)
+                def _():
+                    for kk in range(CORES):
+                        back(dy, pos, kk).start()
+
+                @pl.when(pos == w_own)
+                def _():
+                    back(dy, pos, 1 - k).start()
+                    ret[k, yy, w_own] = res[yy, row]
 
     for copy in sends:
         copy.wait_send()
@@ -279,6 +288,17 @@
         def _():
             for h in range(2):
                 in_plane(i, h).wait_send()
+
+        @pl.when(i != w_own)
+        def _():
+            for dy in range(YS):
+                for kk in range(CORES):
+                    back(dy, i, kk).wait_send()
+
+        @pl.when(i == w_own)
+        def _():
+            for dy in range(YS):
+                back(dy, i, 1 - k).wait_send()
 
     for dy in range(YS):
         yy = lax.rem(y + dy, YS)

time: 41.6 us -> 41.3 us (level)
  no operation moved by 1% of the time
where the time goes in v6:
time: 41.3 us; the launch traced here: 41.2 us
  Pallas kernels  41.1 us (100%)
    pallas_call x1, Pallas kernels, body(): pl.pallas_call(functools.partial(kernel, 1.0 / samples), out_shape=(pltpu...  40.2 us
    pallas_call x1, Pallas kernels, body(): pl.pallas_call(finish, out_shape=jax.ShapeDtypeStruct(shape, F32), in_spe...  0.97 us

profile of v6, /device:TPU:1, one launch (start us, length us, event | category | flops | bytes accessed | tf_op | source)
XLA Modules:
  0.0 41.2 jit_solution(1979502724863147334)
XLA Ops:
  0.0 40.2 %shard_map.28 = (bf16[2,2,8,2,16,128]{5,4,3,2,1,0:T(8,128)(2,1)S(1)}, f32[2,4,8,1024]{3,2,1,0:T(8,128)S(1)}) custom-call(bf16[512,128]{1,0:T(8,128)(2,1)} %bitcast.2, bf16[2,128,16]{2,1,0:T(8,128)(2,1)} %bitcast.3), custom_call_target="tpu_custom_call" | custom-call | tf_op jit(solution)/shard_map/pallas_call | solution.py:366
  40.2 1.0 %shard_map.29 = f32[2,4,8,2048]{3,2,1,0:T(8,128)} custom-call(bf16[2,2,8,2,16,128]{5,4,3,2,1,0:T(8,128)(2,1)S(1)} %get-tuple-element.7.ret, f32[2,4,8,1024]{3,2,1,0:T(8,128)S(1)} %get-tuple-element.8.early), custom_call_target="tpu_custom_call" | custom-call | tf_op jit(solution)/shard_map/pallas_call | solution.py:396
